TPU v7x, 32 devices: a whole 2x2x4 slice. The times are simulated.
32 devices in a mesh: row: 8 (over z, x), col: 4 (over y, core).
Axes of the slice: x: 2, y: 2, z: 4, core: 2. Of those that a mesh axis runs over, the one named last changes fastest.
Arguments:
- krylov_block: bfloat16 [64, 16384], P(None, ('row', 'col')), may hold values from -54 to 54
- degree: int32 [16384], P(('row', 'col')), may hold values from 16 to 64
- tile_values: bfloat16 [256, 4, 64, 512], P('row', 'col'), may hold values from -6 to 6
- tile_column: int32 [256, 4, 8], P('row', 'col'), may hold values from 0 to 63
- tile_live: int32 [256, 4, 8], P('row', 'col'), may hold values 0 or 1
Outputs:
- orthonormal: float32 [64, 16384], P(None, ('row', 'col'))
- quotient: float32 [64, 64], replicated
All inputs are finite; a program needn't handle non-finite values. No bound on the sum of `tile_live` on one device may be relied on, other than what follows from the above.
Results may differ from a plain program's by a relative error of at most 0.0032.
Values may be sent and summed in bfloat16 or wider, within the bound.
No kernel may reach another device: no remote copies, remote signals or barrier semaphores. Data moves between devices by JAX's collectives and lax.ppermute only.
A program may use at most 128 MiB of HBM per device.

v0:
```python
import math
import jax
import jax.numpy as jnp
from jax import lax
from jax.sharding import PartitionSpec as P


def gram_of(left, right):
    return lax.dot_general(
        left,
        right,
        (((1,), (1,)), ((), ())),
        precision=lax.Precision.HIGHEST,
        preferred_element_type=jnp.float32,
    )


def on_device(krylov_block, degree, tile_values, tile_column, tile_live):
    vectors = krylov_block.shape[0]
    owned_rows = krylov_block.shape[1]
    block_rows = tile_values.shape[0]
    height = tile_values.shape[2]
    slot_width = tile_values.shape[3]
    sources = lax.axis_size("row")
    groups = lax.axis_size("col")
    per_piece = owned_rows // height
    inv_root = lax.rsqrt(degree.astype(jnp.float32))
    basis_wide = krylov_block.astype(jnp.float32)
    scaled = (basis_wide * inv_root[None, :]).astype(jnp.bfloat16)
    gathered = lax.all_gather(scaled, "row", axis=1, tiled=True)
    blocks = gathered.reshape(vectors, sources * per_piece, height)
    pick_index = tile_column[:, 0, :].reshape(-1)
    chosen = jnp.take(blocks, pick_index, axis=1)
    chosen = chosen * tile_live[:, 0, :].reshape(1, -1, 1).astype(jnp.bfloat16)
    chosen = chosen.reshape(vectors, block_rows, slot_width)
    panel = tile_values[:, 0]
    whole_rows = jnp.einsum("klc,luc->klu", chosen, panel, preferred_element_type=jnp.float32)
    whole_rows = whole_rows.reshape(vectors, block_rows * height)
    spread = lax.psum_scatter(whole_rows, "col", scatter_dimension=1, tiled=True)
    applied = basis_wide - inv_root[None, :] * spread
    quotient, energy = lax.psum(
        (gram_of(basis_wide, applied), gram_of(applied, applied)), ("row", "col")
    )
    factor = jnp.linalg.cholesky(energy)
    identity = jnp.eye(vectors, dtype=jnp.float32)
    inverse = lax.linalg.triangular_solve(factor, identity, left_side=True, lower=True)
    total_rows = sources * groups * owned_rows
    orthonormal = jnp.dot(inverse, applied, precision=lax.Precision.HIGHEST) * math.sqrt(total_rows)
    return (orthonormal, quotient / total_rows)


def solution(mesh):
    return jax.shard_map(
        on_device,
        mesh=mesh,
        in_specs=(
            P(None, ("row", "col")),
            P(("row", "col")),
            P("row", "col", None, None),
            P("row", "col", None),
            P("row", "col", None),
        ),
        out_specs=(P(None, ("row", "col")), P()),
        check_vma=False,
    )
```

profile of v0, /device:TPU:0, one launch (start us, length us, event | category | flops | bytes accessed | tf_op | source)
XLA Modules:
  0.0 156.6 jit_solution(8631686106743871151)
XLA Ops:
  7.2 0.0 copy-start
  7.2 0.0 reduce-scatter.2.cloned.1.call-start
  7.2 0.9 copy.22
  8.1 0.7 compare_and_fusion
  8.8 0.7 convert_rsqrt_fusion
  9.5 0.9 fusion.8
  10.4 33.0 %all_gather.3 = bf16[64,4096]{1,0:T(8,128)(2,1)S(1)} all-gather(bf16[64,512]{1,0:T(8,128)(2,1)S(1)} %fusion.8), channel_id=1, replica_groups=mesh['row'=8,'col'=4] {'row'}, dimensions={1}, use_global_device_ids=true | all-gather | bytes 589824 | tf_op jit(solution)/shard_map/all_gather | solution.py:30
  43.4 2.1 %reshape.72 = bf16[64,64,64]{2,1,0:T(8,128)(2,1)} reshape(bf16[64,4096]{1,0:T(8,128)(2,1)S(1)} %all_gather.3) | data formatting | bytes 1048576 | tf_op jit(solution)/shard_map/reshape | solution.py:31
  45.5 1.9 %copy.23 = bf16[64,64,64]{2,0,1:T(8,128)(2,1)S(1)} copy(bf16[64,64,64]{2,1,0:T(8,128)(2,1)} %reshape.72) | data formatting | bytes 1048576 | tf_op jit(solution)/shard_map/reshape | solution.py:31
  47.4 0.1 reshape_squeeze.7
  47.5 3.1 %gather_fusion = bf16[256,64,64]{2,1,0:T(8,128)(2,1)} fusion(bf16[64,64,64]{2,0,1:T(8,128)(2,1)S(1)} %copy.23, s32[1024]{0:T(1024)S(1)} %pad_clamp_fusion), kind=kCustom, calls=%fused_computation | custom fusion | bytes 4195328 | tf_op jit(solution)/shard_map/jit(_take)/gather | solution.py:33
  50.6 6.8 %copy.24 = bf16[64,256,64]{2,1,0:T(8,128)(2,1)} copy(bf16[64,256,64]{2,0,1:T(8,128)(2,1)} %bitcast.30) | data formatting | bytes 4194304 | tf_op jit(solution)/shard_map/jit(_take)/gather | solution.py:33
  57.4 0.0 copy-start.2
  57.4 6.5 %gather.7 = bf16[64,32,512]{2,1,0:T(8,128)(2,1)} reshape(bf16[64,256,64]{2,1,0:T(8,128)(2,1)} %copy.24) | data formatting | bytes 4194304 | tf_op jit(solution)/shard_map/jit(_take)/gather | solution.py:33
  63.9 0.0 copy-done.2
  63.9 0.1 copy.25
  64.0 0.1 mul.35
  64.1 0.1 mul.36
  64.2 0.1 copy.21
  64.3 0.1 broadcast_in_dim.18
  64.4 0.1 broadcast_in_dim.19
  64.5 1.8 %select_multiply_fusion = bf16[64,32,512]{2,1,0:T(8,128)(2,1)S(1)} fusion(bf16[64,32,512]{2,1,0:T(8,128)(2,1)} %gather.7, pred[32,512]{1,0:T(8,128)(4,1)S(1)} %broadcast_in_dim.19, bf16[32,512]{1,0:T(8,128)(2,1)S(1)} %mul.36), kind=kLoop, calls=%fused_computation.4 | loop fusion | flops 2097152 | bytes 4243456 | tf_op jit(solution)/shard_map/mul | solution.py:34
  66.3 0.0 copy-done
  66.3 1.4 fusion.3
  67.7 0.0 copy-start.1
  67.7 0.6 copy.27
  68.4 1.1 reshape.73
  69.5 0.0 reduce-scatter.2.cloned.1.call-update
  69.5 22.9 %reduce-scatter.2.cloned.1.call-done = f32[64,512]{1,0:T(8,128)} async-done(((f32[64,2048]{1,0:T(8,128)}), f32[64,512]{1,0:T(8,128)}) %reduce-scatter.2.cloned.1.call-update) | async-done | bytes 131088 | tf_op jit(solution)/shard_map/reduce_scatter | solution.py:39
  92.5 0.0 copy-done.1
  92.5 1.1 convolution_bitcast_fusion
  93.6 1.3 fusion.9
  94.8 40.0 %all-reduce = (f32[64,64]{0,1:T(8,128)S(1)}, f32[64,64]{0,1:T(8,128)S(1)}) all-reduce(f32[64,64]{0,1:T(8,128)S(1)} %fusion.9, f32[64,64]{0,1:T(8,128)S(1)} %convolution_bitcast_fusion), channel_id=1, replica_groups=mesh['row'=8,'col'=4] {'row','col'}, use_global_device_ids=true, to_apply=%region_1.2 | all-reduce | flops 8192 | bytes 65536 | tf_op jit(solution)/shard_map/psum | solution.py:41
  134.8 0.1 copy.29
  134.9 5.8 %cholesky.17 = f32[64,64]{1,0:T(8,128)S(1)} custom-call(f32[64,64]{1,0:T(8,128)S(1)} %fusion.16), custom_call_target="Cholesky" | custom-call | tf_op jit(solution)/shard_map/jit(cholesky)/cholesky | solution.py:44
  140.8 0.6 compare_reduce_fusion
  141.4 0.7 fusion.13
  142.1 4.9 %custom-call.6 = f32[1,64,64]{1,2,0:T(8,128)S(1)} custom-call(f32[1,64,64]{2,1,0:T(8,128)S(1)} %fusion.13), custom_call_target="InvertDiagBlocksLowerTriangular" | custom-call | tf_op jit(solution)/shard_map/triangular_solve | solution.py:46
  147.0 0.2 fusion.14
  147.3 0.7 copy.30
  148.0 1.8 %convolution_multiply_fusion = f32[64,512]{1,0:T(8,128)} fusion(f32[64,64]{1,0:T(8,128)S(1)} %fusion.14, bf16[64,512]{1,0:T(8,128)(2,1)S(1)} %copy-done.1, f32[64,512]{1,0:T(8,128)} %reduce-scatter.2.cloned.1.call-done, f32[512]{0:T(512)S(1)} %convert_rsqrt_fusion), kind=kOutput, calls=%fused_computation.6 | convolution fusion | flops 25296896 | bytes 346112 | tf_op jit(solution)/shard_map/dot_general | solution.py:48
  (6 shorter events, 0.1 us)
Async XLA Ops:
  7.2 59.1 %copy-start = (bf16[32,1,64,512]{3,2,1,0:T(8,128)(2,1)S(1)}, bf16[32,1,64,512]{3,2,1,0:T(8,128)(2,1)}, u32[]{:S(2)}) copy-start(bf16[32,1,64,512]{3,2,1,0:T(8,128)(2,1)} %param.7) | copy-start | bytes 6291460
  7.2 85.3 %reduce-scatter.2.cloned.1.call-start = ((), (), s32[]{:S(2)}) async-start(), calls=%async_computation.1 | async-start | bytes 655360 | tf_op jit(solution)/shard_map/reduce_scatter | solution.py:39
  57.4 6.5 %copy-start.2 = (s32[32,1,8]{0,2,1:T(8,128)S(1)}, s32[32,1,8]{0,2,1:T(8,128)}, u32[]{:S(2)}) copy-start(s32[32,1,8]{0,2,1:T(8,128)} %param.9) | copy-start | bytes 3076
  67.7 24.7 %copy-start.1 = (bf16[64,512]{1,0:T(8,128)(2,1)S(1)}, bf16[64,512]{1,0:T(8,128)(2,1)}, u32[]{:S(2)}) copy-start(bf16[64,512]{1,0:T(8,128)(2,1)} %param.5) | copy-start | bytes 196612
Sparse Core Ops, SparseCore 0:
  69.7 22.7 reduce-scatter.1
where the time goes:
time: 157 us
  blocking collectives  73 us (46%)
  local copies, waits for them, and re-layouts  24.5 us (16%)
  waiting for transfers between devices  22.9 us (15%)
  other arithmetic  16.1 us (10%)
  between operations  14.1 us (9%)
  matrix products  5.85 us (4%)
    psum x1, blocking collectives, on_device(): lax.psum((gram_of(basis_wide, applied), gram_of(applied, applied)), ('row...  40 us
    all_gather x1, blocking collectives, on_device(): gathered = lax.all_gather(scaled, 'row', axis=1, tiled=True)  33 us
    reduce_scatter x1, waiting for transfers between devices, on_device(): lax.psum_scatter(whole_rows, 'col', scatter_dimension=1, tiled=True)  22.9 us
    gather x3, local copies, waits for them, and re-layouts, on_device(): chosen = jnp.take(blocks, pick_index, axis=1)  16.3 us
    another operation x3, other arithmetic, on_device(): factor = jnp.linalg.cholesky(energy)  6.52 us
    another operation x2, other arithmetic, on_device(): lax.linalg.triangular_solve(factor, identity, left_side=True, lower=True)  5.55 us
    reshape x2, local copies, waits for them, and re-layouts, on_device(): blocks = gathered.reshape(vectors, sources * per_piece, height)  4.01 us
  transfers between devices with their start and end apart: 1, of which 1 were waited for; matrix products, arithmetic and copies ran while one was open for 0% of the time, Pallas kernels for 0%

commit v1 on v0

--- a/solution.py
+++ b/solution.py
@@ -27,7 +27,24 @@
     inv_root = lax.rsqrt(degree.astype(jnp.float32))
     basis_wide = krylov_block.astype(jnp.float32)
     scaled = (basis_wide * inv_root[None, :]).astype(jnp.bfloat16)
-    gathered = lax.all_gather(scaled, "row", axis=1, tiled=True)
+    count, place, span = (lax.axis_size("row"), lax.axis_index("row"), scaled.shape[1])
+    right_2 = [(i, (i + 1) % count) for i in range(count)]
+    left_2 = [(i, (i - 1) % count) for i in range(count)]
+    whole = jnp.zeros((*scaled.shape[:1], count * span, *scaled.shape[1 + 1 :]), scaled.dtype)
+    whole = lax.dynamic_update_slice_in_dim(whole, scaled, place * span, axis=1)
+    from_left = from_right = scaled
+    halfway = count // 2
+    for turn in range(1, halfway + 1):
+        from_left = lax.ppermute(from_left, "row", right_2)
+        whole = lax.dynamic_update_slice_in_dim(
+            whole, from_left, (place - turn) % count * span, axis=1
+        )
+        if turn < count - halfway:
+            from_right = lax.ppermute(from_right, "row", left_2)
+            whole = lax.dynamic_update_slice_in_dim(
+                whole, from_right, (place + turn) % count * span, axis=1
+            )
+    gathered = whole
     blocks = gathered.reshape(vectors, sources * per_piece, height)
     pick_index = tile_column[:, 0, :].reshape(-1)
     chosen = jnp.take(blocks, pick_index, axis=1)

time: 157 us -> 148 us (0.943)
  blocking collectives: 73 us -> 40 us
  starting transfers between devices: 0.04 us -> 15.6 us
  waiting for transfers between devices: 22.9 us -> 30.6 us
    all_gather x1 -> x0, blocking collectives: 33 us -> none  [on_device(): gathered = lax.all_gather(scaled, 'row', axis=1, tiled=True)]
    ppermute x0 -> x7, starting transfers between devices: none -> 15.6 us  [the longest x3 12.5 us: on_device(): from_right = lax.ppermute(from_right, 'row', left_2)]
    ppermute x0 -> x7, waiting for transfers between devices: none -> 11.3 us  [the longest x4 11.3 us: on_device(): from_left = lax.ppermute(from_left, 'row', right_2)]
    reduce_scatter x1, waiting for transfers between devices: 22.9 us -> 19.3 us  [on_device(): lax.psum_scatter(whole_rows, 'col', scatter_dimension=1, tiled=True)]
  transfers between devices with their start and end apart: 1 -> 8, of which waited for: 1 -> 4; matrix products, arithmetic and copies ran while one was open for 0% -> 2% of each run, Pallas kernels for 0% -> 0%
where the time goes in v1:
time: 148 us
  blocking collectives  40 us (27%)
  waiting for transfers between devices  30.6 us (21%)
  local copies, waits for them, and re-layouts  24.5 us (17%)
  other arithmetic  17 us (11%)
  starting transfers between devices  15.6 us (11%)
  between operations  14.3 us (10%)
  matrix products  5.85 us (4%)
    psum x1, blocking collectives, on_device(): lax.psum((gram_of(basis_wide, applied), gram_of(applied, applied)), ('row...  40 us
    reduce_scatter x1, waiting for transfers between devices, on_device(): lax.psum_scatter(whole_rows, 'col', scatter_dimension=1, tiled=True)  19.3 us
    gather x3, local copies, waits for them, and re-layouts, on_device(): chosen = jnp.take(blocks, pick_index, axis=1)  16.3 us
    ppermute x3, starting transfers between devices, on_device(): from_right = lax.ppermute(from_right, 'row', left_2)  12.5 us
    ppermute x4, waiting for transfers between devices, on_device(): from_left = lax.ppermute(from_left, 'row', right_2)  11.3 us
    another operation x3, other arithmetic, on_device(): factor = jnp.linalg.cholesky(energy)  6.52 us
    another operation x2, other arithmetic, on_device(): lax.linalg.triangular_solve(factor, identity, left_side=True, lower=True)  5.55 us
    reshape x2, local copies, waits for them, and re-layouts, on_device(): blocks = gathered.reshape(vectors, sources * per_piece, height)  3.99 us
  transfers between devices with their start and end apart: 8, of which 4 were waited for; matrix products, arithmetic and copies ran while one was open for 2% of the time, Pallas kernels for 0%

profile of v1, /device:TPU:0, one launch (start us, length us, event | category | flops | bytes accessed | tf_op | source)
XLA Modules:
  0.0 147.8 jit_solution(4958539220924424243)
XLA Ops:
  7.2 0.0 copy-start
  7.2 0.0 reduce-scatter.2.cloned.1.call-start
  7.2 0.8 convert_rsqrt_fusion
  8.1 0.9 constant_dynamic-update-slice_fusion.7
  9.0 3.0 %collective-permute-start = (bf16[64,512]{1,0:T(8,128)(2,1)S(1)}, bf16[64,512]{1,0:T(8,128)(2,1)S(1)}, u32[]{:S(2)}, u32[]{:S(2)}) collective-permute-start(bf16[64,512]{1,0:T(8,128)(2,1)S(1)} %get-tuple-element.11), channel_id=1, source_target_pairs={{0,4},{4,8},{8,12},{12,16},{16,20},{20,24},{24,28},{28,0},{1,5},{5... | collective-permute-start | bytes 196616 | tf_op jit(solution)/shard_map/ppermute | solution.py:38
  12.0 3.1 %collective-permute-start.1 = (bf16[64,512]{1,0:T(8,128)(2,1)S(1)}, bf16[64,512]{1,0:T(8,128)(2,1)S(1)}, u32[]{:S(2)}, u32[]{:S(2)}) collective-permute-start(bf16[64,512]{1,0:T(8,128)(2,1)S(1)} %get-tuple-element.11), channel_id=1, source_target_pairs={{0,28},{4,0},{8,4},{12,8},{16,12},{20,16},{24,20},{28,24},{1,29},{... | collective-permute-start | bytes 196616 | tf_op jit(solution)/shard_map/ppermute | solution.py:43
  15.1 0.8 copy.22
  15.8 0.7 compare_and_fusion
  16.5 0.1 reshape_squeeze.7
  16.6 0.7 convert_bitcast_fusion
  17.3 0.1 copy.25
  17.4 0.1 mul.67
  17.5 0.1 mul.68
  17.6 0.1 copy.21
  17.7 0.1 broadcast_in_dim.21
  17.8 0.1 broadcast_in_dim.22
  18.0 0.0 collective-permute-done
  18.0 0.1 collective-permute-start.2
  18.1 0.0 collective-permute-done.1
  18.1 4.7 %collective-permute-start.3 = (bf16[64,512]{1,0:T(8,128)(2,1)S(1)}, bf16[64,512]{1,0:T(8,128)(2,1)S(1)}, u32[]{:S(2)}, u32[]{:S(2)}) collective-permute-start(bf16[64,512]{1,0:T(8,128)(2,1)S(1)} %collective-permute-done.1), channel_id=1, source_target_pairs={{0,28},{4,0},{8,4},{12,8},{16,12},{20,16},{24,20},{28,24},{1,29},{... | collective-permute-start | bytes 196616 | tf_op jit(solution)/shard_map/ppermute | solution.py:43
  22.8 2.2 %collective-permute-done.2 = bf16[64,512]{1,0:T(8,128)(2,1)S(1)} collective-permute-done((bf16[64,512]{1,0:T(8,128)(2,1)S(1)}, bf16[64,512]{1,0:T(8,128)(2,1)S(1)}, u32[]{:S(2)}, u32[]{:S(2)}) %collective-permute-start.2) | collective-permute-done | bytes 65568 | tf_op jit(solution)/shard_map/ppermute | solution.py:38
  25.0 0.0 collective-permute-done.3
  25.0 4.7 %collective-permute-start.5 = (bf16[64,512]{1,0:T(8,128)(2,1)S(1)}, bf16[64,512]{1,0:T(8,128)(2,1)S(1)}, u32[]{:S(2)}, u32[]{:S(2)}) collective-permute-start(bf16[64,512]{1,0:T(8,128)(2,1)S(1)} %collective-permute-done.3), channel_id=1, source_target_pairs={{0,28},{4,0},{8,4},{12,8},{16,12},{20,16},{24,20},{28,24},{1,29},{... | collective-permute-start | bytes 196616 | tf_op jit(solution)/shard_map/ppermute | solution.py:43
  29.8 2.2 %collective-permute-done.4 = bf16[64,512]{1,0:T(8,128)(2,1)S(1)} collective-permute-done((bf16[64,512]{1,0:T(8,128)(2,1)S(1)}, bf16[64,512]{1,0:T(8,128)(2,1)S(1)}, u32[]{:S(2)}, u32[]{:S(2)}) %collective-permute-start.4) | collective-permute-done | bytes 65568 | tf_op jit(solution)/shard_map/ppermute | solution.py:38
  32.0 0.0 collective-permute-start.6
  32.0 6.9 %collective-permute-done.6 = bf16[64,512]{1,0:T(8,128)(2,1)S(1)} collective-permute-done((bf16[64,512]{1,0:T(8,128)(2,1)S(1)}, bf16[64,512]{1,0:T(8,128)(2,1)S(1)}, u32[]{:S(2)}, u32[]{:S(2)}) %collective-permute-start.6) | collective-permute-done | bytes 65568 | tf_op jit(solution)/shard_map/ppermute | solution.py:38
  39.0 2.1 %reshape.72 = bf16[64,64,64]{2,1,0:T(8,128)(2,1)} reshape(bf16[64,4096]{1,0:T(8,128)(2,1)S(1)} %constant_dynamic-update-slice_fusion) | data formatting | bytes 1048576 | tf_op jit(solution)/shard_map/reshape | solution.py:48
  41.0 1.9 %copy.23 = bf16[64,64,64]{2,0,1:T(8,128)(2,1)S(1)} copy(bf16[64,64,64]{2,1,0:T(8,128)(2,1)} %reshape.72) | data formatting | bytes 1048576 | tf_op jit(solution)/shard_map/reshape | solution.py:48
  43.0 3.1 %gather_fusion = bf16[256,64,64]{2,1,0:T(8,128)(2,1)} fusion(bf16[64,64,64]{2,0,1:T(8,128)(2,1)S(1)} %copy.23, s32[1024]{0:T(1024)S(1)} %pad_clamp_fusion), kind=kCustom, calls=%fused_computation | custom fusion | bytes 4195328 | tf_op jit(solution)/shard_map/jit(_take)/gather | solution.py:50
  46.0 6.8 %copy.24 = bf16[64,256,64]{2,1,0:T(8,128)(2,1)} copy(bf16[64,256,64]{2,0,1:T(8,128)(2,1)} %bitcast.30) | data formatting | bytes 4194304 | tf_op jit(solution)/shard_map/jit(_take)/gather | solution.py:50
  52.8 6.4 %gather.7 = bf16[64,32,512]{2,1,0:T(8,128)(2,1)} reshape(bf16[64,256,64]{2,1,0:T(8,128)(2,1)} %copy.24) | data formatting | bytes 4194304 | tf_op jit(solution)/shard_map/jit(_take)/gather | solution.py:50
  59.3 1.8 %select_multiply_fusion = bf16[64,32,512]{2,1,0:T(8,128)(2,1)S(1)} fusion(bf16[64,32,512]{2,1,0:T(8,128)(2,1)} %gather.7, pred[32,512]{1,0:T(8,128)(4,1)S(1)} %broadcast_in_dim.22, bf16[32,512]{1,0:T(8,128)(2,1)S(1)} %mul.68), kind=kLoop, calls=%fused_computation.4 | loop fusion | flops 2097152 | bytes 4243456 | tf_op jit(solution)/shard_map/mul | solution.py:51
  61.1 1.4 fusion.3
  62.5 0.6 copy.27
  63.1 1.2 reshape.73
  64.3 0.0 reduce-scatter.2.cloned.1.call-update
  64.3 19.3 %reduce-scatter.2.cloned.1.call-done = f32[64,512]{1,0:T(8,128)} async-done(((f32[64,2048]{1,0:T(8,128)}), f32[64,512]{1,0:T(8,128)}) %reduce-scatter.2.cloned.1.call-update) | async-done | bytes 131088 | tf_op jit(solution)/shard_map/reduce_scatter | solution.py:56
  83.6 1.1 convolution_bitcast_fusion
  84.7 1.3 fusion.9
  85.9 40.0 %all-reduce = (f32[64,64]{0,1:T(8,128)S(1)}, f32[64,64]{0,1:T(8,128)S(1)}) all-reduce(f32[64,64]{0,1:T(8,128)S(1)} %fusion.9, f32[64,64]{0,1:T(8,128)S(1)} %convolution_bitcast_fusion), channel_id=1, replica_groups=mesh['row'=8,'col'=4] {'row','col'}, use_global_device_ids=true, to_apply=%region_1.2 | all-reduce | flops 8192 | bytes 65536 | tf_op jit(solution)/shard_map/psum | solution.py:58
  126.0 0.1 copy.29
  126.1 5.8 %cholesky.17 = f32[64,64]{1,0:T(8,128)S(1)} custom-call(f32[64,64]{1,0:T(8,128)S(1)} %fusion.16), custom_call_target="Cholesky" | custom-call | tf_op jit(solution)/shard_map/jit(cholesky)/cholesky | solution.py:61
  131.9 0.6 compare_reduce_fusion
  132.6 0.7 fusion.13
  133.2 4.9 %custom-call.6 = f32[1,64,64]{1,2,0:T(8,128)S(1)} custom-call(f32[1,64,64]{2,1,0:T(8,128)S(1)} %fusion.13), custom_call_target="InvertDiagBlocksLowerTriangular" | custom-call | tf_op jit(solution)/shard_map/triangular_solve | solution.py:63
  138.1 0.2 fusion.14
  138.4 0.7 copy.30
  139.1 1.8 %convolution_multiply_fusion = f32[64,512]{1,0:T(8,128)} fusion(f32[64,64]{1,0:T(8,128)S(1)} %fusion.14, bf16[64,512]{1,0:T(8,128)(2,1)S(1)} %copy-done.1, f32[64,512]{1,0:T(8,128)} %reduce-scatter.2.cloned.1.call-done, f32[512]{0:T(512)S(1)} %convert_rsqrt_fusion), kind=kOutput, calls=%fused_computation.6 | convolution fusion | flops 25296896 | bytes 346112 | tf_op jit(solution)/shard_map/dot_general | solution.py:65
  (18 shorter events, 0.2 us)
Async XLA Ops:
  7.2 53.9 %copy-start = (bf16[32,1,64,512]{3,2,1,0:T(8,128)(2,1)S(1)}, bf16[32,1,64,512]{3,2,1,0:T(8,128)(2,1)}, u32[]{:S(2)}) copy-start(bf16[32,1,64,512]{3,2,1,0:T(8,128)(2,1)} %param.7) | copy-start | bytes 6291460
  7.2 76.4 %reduce-scatter.2.cloned.1.call-start = ((), (), s32[]{:S(2)}) async-start(), calls=%async_computation.1 | async-start | bytes 655360 | tf_op jit(solution)/shard_map/reduce_scatter | solution.py:56
  9.0 9.0 %collective-permute-start = (bf16[64,512]{1,0:T(8,128)(2,1)S(1)}, bf16[64,512]{1,0:T(8,128)(2,1)S(1)}, u32[]{:S(2)}, u32[]{:S(2)}) collective-permute-start(bf16[64,512]{1,0:T(8,128)(2,1)S(1)} %get-tuple-element.11), channel_id=1, source_target_pairs={{0,4},{4,8},{8,12},{12,16},{16,20},{20,24},{24,28},{28,0},{1,5},{5... | collective-permute-start | bytes 196616 | tf_op jit(solution)/shard_map/ppermute | solution.py:38
  12.0 6.1 %collective-permute-start.1 = (bf16[64,512]{1,0:T(8,128)(2,1)S(1)}, bf16[64,512]{1,0:T(8,128)(2,1)S(1)}, u32[]{:S(2)}, u32[]{:S(2)}) collective-permute-start(bf16[64,512]{1,0:T(8,128)(2,1)S(1)} %get-tuple-element.11), channel_id=1, source_target_pairs={{0,28},{4,0},{8,4},{12,8},{16,12},{20,16},{24,20},{28,24},{1,29},{... | collective-permute-start | bytes 196616 | tf_op jit(solution)/shard_map/ppermute | solution.py:43
  18.0 7.0 %collective-permute-start.2 = (bf16[64,512]{1,0:T(8,128)(2,1)S(1)}, bf16[64,512]{1,0:T(8,128)(2,1)S(1)}, u32[]{:S(2)}, u32[]{:S(2)}) collective-permute-start(bf16[64,512]{1,0:T(8,128)(2,1)S(1)} %collective-permute-done), channel_id=1, source_target_pairs={{0,4},{4,8},{8,12},{12,16},{16,20},{20,24},{24,28},{28,0},{1,5},{5... | collective-permute-start | bytes 196616 | tf_op jit(solution)/shard_map/ppermute | solution.py:38
  18.1 6.9 %collective-permute-start.3 = (bf16[64,512]{1,0:T(8,128)(2,1)S(1)}, bf16[64,512]{1,0:T(8,128)(2,1)S(1)}, u32[]{:S(2)}, u32[]{:S(2)}) collective-permute-start(bf16[64,512]{1,0:T(8,128)(2,1)S(1)} %collective-permute-done.1), channel_id=1, source_target_pairs={{0,28},{4,0},{8,4},{12,8},{16,12},{20,16},{24,20},{28,24},{1,29},{... | collective-permute-start | bytes 196616 | tf_op jit(solution)/shard_map/ppermute | solution.py:43
  25.0 7.0 %collective-permute-start.4 = (bf16[64,512]{1,0:T(8,128)(2,1)S(1)}, bf16[64,512]{1,0:T(8,128)(2,1)S(1)}, u32[]{:S(2)}, u32[]{:S(2)}) collective-permute-start(bf16[64,512]{1,0:T(8,128)(2,1)S(1)} %collective-permute-done.2), channel_id=1, source_target_pairs={{0,4},{4,8},{8,12},{12,16},{16,20},{20,24},{24,28},{28,0},{1,5},{5... | collective-permute-start | bytes 196616 | tf_op jit(solution)/shard_map/ppermute | solution.py:38
  25.0 7.0 %collective-permute-start.5 = (bf16[64,512]{1,0:T(8,128)(2,1)S(1)}, bf16[64,512]{1,0:T(8,128)(2,1)S(1)}, u32[]{:S(2)}, u32[]{:S(2)}) collective-permute-start(bf16[64,512]{1,0:T(8,128)(2,1)S(1)} %collective-permute-done.3), channel_id=1, source_target_pairs={{0,28},{4,0},{8,4},{12,8},{16,12},{20,16},{24,20},{28,24},{1,29},{... | collective-permute-start | bytes 196616 | tf_op jit(solution)/shard_map/ppermute | solution.py:43
  32.0 7.0 %collective-permute-start.6 = (bf16[64,512]{1,0:T(8,128)(2,1)S(1)}, bf16[64,512]{1,0:T(8,128)(2,1)S(1)}, u32[]{:S(2)}, u32[]{:S(2)}) collective-permute-start(bf16[64,512]{1,0:T(8,128)(2,1)S(1)} %collective-permute-done.4), channel_id=1, source_target_pairs={{0,4},{4,8},{8,12},{12,16},{16,20},{20,24},{24,28},{28,0},{1,5},{5... | collective-permute-start | bytes 196616 | tf_op jit(solution)/shard_map/ppermute | solution.py:38
  62.5 21.1 %copy-start.1 = (bf16[64,512]{1,0:T(8,128)(2,1)S(1)}, bf16[64,512]{1,0:T(8,128)(2,1)}, u32[]{:S(2)}) copy-start(bf16[64,512]{1,0:T(8,128)(2,1)} %param.5) | copy-start | bytes 196612
Sparse Core Ops, SparseCore 0:
  64.4 19.0 reduce-scatter.1
